TPU v7x, 256 devices: a whole 4x4x8 slice. The times are simulated.
256 devices in a mesh: user: 32 (over y, z_hi, core), item: 8 (over x, z_lo).
Axes of the slice: x: 4, y: 4, z: 8 (z_hi: 4, z_lo: 2; z = z_hi * 2 + z_lo), core: 2. Of those that a mesh axis runs over, the one named last changes fastest.
Arguments:
- observed: bfloat16 [256, 128, 128, 128], P(('user', 'item')), may hold values from -6 to 6
- user_block: int32 [256], P(('user', 'item')), may hold values from 0 to 3
- item_block: int32 [256], P(('user', 'item')), may hold values from 0 to 1
- stratum: int32 [256], P(('user', 'item')), may hold values from 0 to 7
- context_ids: int32 [256, 128], P(('user', 'item')), may hold values from 0 to 2047
- core_tensor: float32 [16384, 128], P(('user', 'item')), may hold values from -1 to 1
- user_factor: bfloat16 [16384, 128], P('user'), may hold values from -3 to 3
- item_factor: bfloat16 [2048, 128], P('item'), may hold values from -3 to 3
- context_factor: bfloat16 [2048, 128], P(('user', 'item')), may hold values from -3 to 3
Outputs:
- core_grad: float32 [16384, 128], P(('user', 'item'))
- user_grad: float32 [16384, 128], P(('user', 'item'))
- item_grad: float32 [2048, 128], P(('user', 'item'))
- context_grad: float32 [2048, 128], P(('user', 'item'))
Inputs may be any that keep to these rules, and one draw needn't show every extreme that they name: `user_block`: user block within the tile's user index.
All inputs are finite; a program needn't handle non-finite values.
Results may differ from a plain program's by a relative error of at most 0.0031.
Values may be sent and summed in bfloat16 or wider, within the bound.
No kernel may reach another device: no remote copies, remote signals or barrier semaphores. Data moves between devices by JAX's collectives and lax.ppermute only.
A program may use at most 128 MiB of HBM per device.

v0:
```python
import math

import jax
import jax.numpy as jnp
from jax import lax
from jax.sharding import PartitionSpec as P


def contract_last(left, right):
    return lax.dot_general(
        left, right, (((1,), (1,)), ((), ())), preferred_element_type=jnp.float32
    )


def contract_first(left, right):
    return lax.dot_general(
        left, right, (((0,), (0,)), ((), ())), preferred_element_type=jnp.float32
    )


def tile_terms(core_half, user_rows, item_rows, ctx_rows, observed_tile):
    rank_one = user_rows.shape[1]
    rank_two = item_rows.shape[1]
    block_user, block_item, slices = observed_tile.shape
    first_pass = contract_last(core_half, ctx_rows).astype(jnp.bfloat16)
    first_cube = first_pass.reshape(rank_one, rank_two, slices)
    second = jnp.einsum(
        "pqc,bq->pbc", first_cube, item_rows, preferred_element_type=jnp.float32
    ).astype(jnp.bfloat16)
    second_flat = second.reshape(rank_one, block_item * slices)
    predicted = jnp.dot(user_rows, second_flat, preferred_element_type=jnp.float32)
    residual = (
        predicted - observed_tile.reshape(block_user, block_item * slices).astype(jnp.float32)
    ).astype(jnp.bfloat16)
    grad_user = contract_last(residual, second_flat)
    back_flat = contract_first(user_rows, residual).astype(jnp.bfloat16)
    back_cube = back_flat.reshape(rank_one, block_item, slices)
    grad_item = jnp.einsum("pbc,pqc->bq", back_cube, first_cube, preferred_element_type=jnp.float32)
    folded = jnp.einsum(
        "pbc,bq->pqc", back_cube, item_rows, preferred_element_type=jnp.float32
    ).astype(jnp.bfloat16)
    folded = folded.reshape(rank_one * rank_two, slices)
    grad_ctx = contract_first(folded, core_half)
    grad_core = jnp.dot(folded, ctx_rows, preferred_element_type=jnp.float32)
    return (grad_core, grad_user, grad_item, grad_ctx)


def local(
    observed,
    user_block,
    item_block,
    stratum,
    context_ids,
    core_tensor,
    user_factor,
    item_factor,
    context_factor,
):
    core_half = core_tensor.astype(jnp.bfloat16)
    item_all = lax.all_gather(item_factor, "item", axis=0, tiled=True)
    core_all, context_all = (
        lax.all_gather(core_half, ("user", "item"), axis=0, tiled=True),
        lax.all_gather(context_factor, ("user", "item"), axis=0, tiled=True),
    )
    tiles_here, block_user, block_item, slices = observed.shape
    blocks_stratum = item_factor.shape[0] // block_item
    count_ctx = context_all.shape[0]
    scale = 1.0 / math.sqrt(block_user * block_item * slices)
    columns = jnp.arange(count_ctx, dtype=jnp.int32)

    def one_tile(index, carry):
        acc_core, acc_user, acc_item, acc_ctx = carry
        user_start = user_block[index] * block_user
        item_start = (stratum[index] * blocks_stratum + item_block[index]) * block_item
        user_rows = lax.dynamic_slice_in_dim(user_factor, user_start, block_user, 0)
        item_rows = lax.dynamic_slice_in_dim(item_all, item_start, block_item, 0)
        slice_ids = context_ids[index]
        ctx_rows = jnp.take(context_all, slice_ids, axis=0)
        g_core, g_user, g_item, g_ctx = tile_terms(
            core_all, user_rows, item_rows, ctx_rows, observed[index]
        )
        old_user = lax.dynamic_slice_in_dim(acc_user, user_start, block_user, 0)
        acc_user = lax.dynamic_update_slice_in_dim(acc_user, old_user + g_user, user_start, 0)
        old_item = lax.dynamic_slice_in_dim(acc_item, item_start, block_item, 0)
        acc_item = lax.dynamic_update_slice_in_dim(acc_item, old_item + g_item, item_start, 0)
        picker = (slice_ids[:, None] == columns[None, :]).astype(jnp.float32)
        acc_ctx = acc_ctx + lax.dot_general(
            picker,
            g_ctx,
            (((0,), (0,)), ((), ())),
            precision=lax.Precision.HIGHEST,
            preferred_element_type=jnp.float32,
        )
        return (acc_core + g_core, acc_user, acc_item, acc_ctx)

    init = (
        jnp.zeros(core_all.shape, jnp.float32),
        jnp.zeros(user_factor.shape, jnp.float32),
        jnp.zeros(item_all.shape, jnp.float32),
        jnp.zeros(context_all.shape, jnp.float32),
    )
    acc_core, acc_user, acc_item, acc_ctx = lax.fori_loop(0, tiles_here, one_tile, init)
    term_core = acc_core * scale
    term_user = acc_user * scale
    term_item = acc_item * scale
    term_ctx = acc_ctx * scale
    core_grad, item_grad, context_grad = (
        lax.psum_scatter(term_core, ("user", "item"), scatter_dimension=0, tiled=True),
        lax.psum_scatter(term_item, ("user", "item"), scatter_dimension=0, tiled=True),
        lax.psum_scatter(term_ctx, ("user", "item"), scatter_dimension=0, tiled=True),
    )
    user_grad = lax.psum_scatter(term_user, "item", scatter_dimension=0, tiled=True)
    return (core_grad, user_grad, item_grad, context_grad)


def solution(mesh):
    return jax.shard_map(
        local,
        mesh=mesh,
        in_specs=(
            P(("user", "item"), None, None, None),
            P(("user", "item")),
            P(("user", "item")),
            P(("user", "item")),
            P(("user", "item"), None),
            P(("user", "item"), None),
            P("user", None),
            P("item", None),
            P(("user", "item"), None),
        ),
        out_specs=(
            P(("user", "item"), None),
            P(("user", "item"), None),
            P(("user", "item"), None),
            P(("user", "item"), None),
        ),
        check_vma=False,
    )
```

profile of v0, /device:TPU:0, one launch (start us, length us, event | category | flops | bytes accessed | tf_op | source)
XLA Modules:
  0.0 2378.1 jit_solution(11638213165821994805)
XLA Ops:
  7.2 1.4 convert_element_type.41
  10.7 6.5 convert.2
  17.2 630.0 %all_gather.10 = bf16[2048,128]{1,0:T(8,128)(2,1)S(1)} all-gather(bf16[8,128]{1,0:T(8,128)(2,1)S(1)} %copy-done.6), channel_id=1, replica_groups=mesh['user'=32,'item'=8] {'user','item'}, dimensions={0}, use_global_device_ids=true | all-gather | bytes 526336 | tf_op jit(solution)/shard_map/all_gather | solution.py:63
  648.0 29.5 %all_gather.9 = bf16[2048,128]{1,0:T(8,128)(2,1)S(1)} all-gather(bf16[256,128]{1,0:T(8,128)(2,1)S(1)} %copy-done.5), channel_id=1, replica_groups=mesh['user'=32,'item'=8] {'item'}, dimensions={0}, use_global_device_ids=true | all-gather | bytes 589824 | tf_op jit(solution)/shard_map/all_gather | solution.py:60
  677.5 56.4 %all-gather.2.cloned.1.call-done = bf16[16384,128]{1,0:T(8,128)(2,1)} async-done(((bf16[64,128]{1,0:T(8,128)(2,1)}), bf16[16384,128]{1,0:T(8,128)(2,1)}) %all-gather.2.cloned.1.call-update) | async-done | bytes 4194320 | tf_op jit(solution)/shard_map/all_gather | solution.py:62
  733.8 3.6 fusion.15
  737.5 1.3 fusion.12
  738.8 0.9 slice-done.1
  739.6 18.2 fusion
  757.9 1.3 fusion.16
  759.9 1.2 copy.26
  761.1 1.3 convolution_convert_fusion.2
  762.5 1.3 fusion.23
  763.9 1.1 broadcast_multiply_fusion
  765.0 1.5 copy-done.2
  766.5 1.4 fusion.40
  767.8 2.0 convolution_multiply_fusion.1
  770.0 7.9 fusion.17
  777.9 0.7 broadcast_multiply_fusion.1
  778.7 6.8 convolution_multiply_fusion
  785.6 247.0 %all-reduce.5.cloned.1.call-done = (f32[2048,128]{1,0:T(8,128)}, f32[2048,128]{1,0:T(8,128)}) async-done(((f32[2048,128]{1,0:T(8,128)}, f32[2048,128]{1,0:T(8,128)}), (f32[2048,128]{1,0:T(8,128)}, f32[2048,128]{1,0:T(8,128)})) %all-reduce.5.cloned.1.call-update) | async-done | bytes 2097168
  1032.6 1.3 constant_dynamic-slice_fusion
  1033.8 41.2 %reduce-scatter.5.cloned.1.call-done = f32[64,128]{1,0:T(8,128)} async-done(((f32[512,128]{1,0:T(8,128)}), f32[64,128]{1,0:T(8,128)}) %reduce-scatter.5.cloned.1.call-update) | async-done | bytes 32784 | tf_op jit(solution)/shard_map/reduce_scatter | solution.py:112
  1075.0 1296.6 %reduce-scatter.3.cloned.1.call-done = f32[64,128]{1,0:T(8,128)} async-done(((f32[16384,128]{1,0:T(8,128)}), f32[64,128]{1,0:T(8,128)}) %reduce-scatter.3.cloned.1.call-update) | async-done | bytes 32784 | tf_op jit(solution)/shard_map/reduce_scatter | solution.py:108
  (33 shorter events, 1.8 us)
Async XLA Ops:
  7.2 731.6 %copy-start = (bf16[512,128]{1,0:T(8,128)(2,1)S(1)}, bf16[512,128]{1,0:T(8,128)(2,1)}, u32[]{:S(2)}) copy-start(bf16[512,128]{1,0:T(8,128)(2,1)} %param.15) | copy-start | bytes 393220
  7.2 726.6 %all-gather.2.cloned.1.call-start = ((), (), s32[]{:S(2)}) async-start(), calls=%async_computation.2 | async-start | bytes 4210688 | tf_op jit(solution)/shard_map/all_gather | solution.py:62
  8.6 1023.9 %all-reduce.5.cloned.1.call-start = ((), (), s32[]{:S(2)}) async-start(), calls=%async_computation.5 | async-start | bytes 4194304
  10.6 6.6 copy-start.7
  10.7 6.6 copy-start.6
  10.7 637.3 %copy-start.5 = (bf16[256,128]{1,0:T(8,128)(2,1)S(1)}, bf16[256,128]{1,0:T(8,128)(2,1)}, u32[]{:S(2)}) copy-start(bf16[256,128]{1,0:T(8,128)(2,1)} %param.16) | copy-start | bytes 196612
  733.8 4.9 slice-start
  737.4 2.2 slice-start.1
  738.7 19.2 copy-start.3
  757.9 2.0 copy-start.4
  762.4 2.6 copy-start.1
  762.5 4.0 copy-start.2
  769.9 305.1 %reduce-scatter.5.cloned.1.call-start = ((), (), s32[]{:S(2)}) async-start(), calls=%async_computation.4 | async-start | bytes 294912 | tf_op jit(solution)/shard_map/reduce_scatter | solution.py:112
  778.7 1592.9 %reduce-scatter.3.cloned.1.call-start = ((), (), s32[]{:S(2)}) async-start(), calls=%async_computation.3 | async-start | bytes 8421376 | tf_op jit(solution)/shard_map/reduce_scatter | solution.py:108
Sparse Core Ops, SparseCore 0:
  10.4 723.3 all-gather.1
  770.0 262.4 all-reduce.4
  1035.6 39.3 reduce-scatter.4
  1077.9 1293.5 reduce-scatter.2
where the time goes:
time: 2380 us
  waiting for transfers between devices  1640 us (69%)
  blocking collectives  659 us (28%)
  matrix products  45.2 us (2%)
    reduce_scatter x1, waiting for transfers between devices, local(): lax.psum_scatter(term_core, ('user', 'item'), scatter_dimension=0, tiled=...  1300 us
    all_gather x1, blocking collectives, local(): lax.all_gather(context_factor, ('user', 'item'), axis=0, tiled=True)  630 us
    unnamed x5, waiting for transfers between devices  247 us
    all_gather x1, waiting for transfers between devices, local(): lax.all_gather(core_half, ('user', 'item'), axis=0, tiled=True)  56.4 us
  transfers between devices with their start and end apart: 4, of which 4 were waited for; matrix products, arithmetic and copies ran while one was open for 1% of the time, Pallas kernels for 0%

commit v1 on v0

v1 whole, which is shorter than its diff:
```python
import math

import jax
import jax.numpy as jnp
from jax import lax
from jax.sharding import Mesh, PartitionSpec as P

BF = jnp.bfloat16
F32 = jnp.float32
ALL = ("y", "zh", "core", "x", "zl")
BIG = ("y", "x", "zl")
CORE_ROWS, CTX_ROWS, ITEM_ROWS = 64, 8, 8
ROWS = CORE_ROWS + CTX_ROWS + ITEM_ROWS


def dot_nt(left, right, precision=None):
    return lax.dot_general(
        left, right, (((1,), (1,)), ((), ())), precision=precision, preferred_element_type=F32
    )


def dot_tn(left, right):
    return lax.dot_general(left, right, (((0,), (0,)), ((), ())), preferred_element_type=F32)


def swap(value):
    return lax.ppermute(value, "core", [(0, 1), (1, 0)])


def gather_all(block):
    one = lax.all_to_all(
        jnp.broadcast_to(block[None], (4,) + block.shape), "zh", 0, 0, tiled=True
    )
    own = lax.all_to_all(
        jnp.broadcast_to(one[None], (32,) + one.shape), BIG, 0, 0, tiled=True
    ).reshape(4, 4, 2, 4, ROWS, 128)
    return own, swap(own)


def reduce_all(own, other):
    both = (own + swap(other).astype(F32)).astype(BF)
    parts = lax.all_to_all(both.reshape(32, 4, ROWS, 128), BIG, 0, 0, tiled=True)
    some = jnp.sum(parts.astype(F32), axis=0)
    last = lax.all_to_all(some, "zh", 0, 0, tiled=True)
    return jnp.sum(last, axis=0)


def tile_terms(core_half, user_rows, item_rows, ctx_rows, observed):
    rank_one = user_rows.shape[1]
    rank_two = item_rows.shape[1]
    block_user, block_item, slices = observed.shape
    first = dot_nt(core_half, ctx_rows).astype(BF)
    first_cube = first.reshape(rank_one, rank_two, slices)
    second = jnp.einsum(
        "pqc,bq->pbc", first_cube, item_rows, preferred_element_type=F32
    ).astype(BF)
    second_flat = second.reshape(rank_one, block_item * slices)
    predicted = jnp.dot(user_rows, second_flat, preferred_element_type=F32)
    residual = (predicted - observed.reshape(block_user, -1).astype(F32)).astype(BF)
    grad_user = dot_nt(residual, second_flat)
    back = dot_tn(user_rows, residual).astype(BF).reshape(rank_one, block_item, slices)
    grad_item = jnp.einsum("pbc,pqc->bq", back, first_cube, preferred_element_type=F32)
    folded = jnp.einsum("pbc,bq->pqc", back, item_rows, preferred_element_type=F32)
    folded = folded.astype(BF).reshape(rank_one * rank_two, slices)
    grad_ctx = dot_tn(folded, core_half)
    grad_core = jnp.dot(folded, ctx_rows, preferred_element_type=F32)
    return grad_core, grad_user, grad_item, grad_ctx


def local(
    observed,
    user_block,
    item_block,
    stratum,
    context_ids,
    core_tensor,
    user_factor,
    item_factor,
    context_factor,
):
    y, zh, core, x, zl = (lax.axis_index(name) for name in ALL)
    scale = 1.0 / math.sqrt(128 * 128 * 128)
    ub, ib, st, ids = user_block[0], item_block[0], stratum[0], context_ids[0]
    mine = (y * 4 + zh) * 2 + core
    item_own = lax.dynamic_slice_in_dim(item_factor, mine * ITEM_ROWS, ITEM_ROWS, 0)
    block = jnp.concatenate([core_tensor.astype(BF), context_factor, item_own], axis=0)
    own, other = gather_all(block)
    both = jnp.stack([own, other])

    core_half = both[..., :CORE_ROWS, :].transpose(0, 1, 4, 2, 3, 5, 6).reshape(16384, 128)
    def spot_of(row):
        j, d = row & 7, row >> 3
        d_zl, d_x, d_c, d_zh, d_y = d & 1, (d >> 1) & 3, (d >> 3) & 1, (d >> 4) & 3, d >> 6
        place = ((((d_c ^ core) * 4 + d_y) * 4 + d_x) * 2 + d_zl) * 4 + d_zh
        return place * 8 + j

    spot = spot_of(ids)
    item_spot = spot_of((st * 2 + ib) * 128 + jnp.arange(128, dtype=jnp.int32))
    ctx_table = both[..., CORE_ROWS : CORE_ROWS + CTX_ROWS, :].reshape(2048, 128)
    ctx_rows = jnp.take(ctx_table, spot, axis=0)
    item_table = both[..., CORE_ROWS + CTX_ROWS :, :]
    picked = lax.dynamic_slice(
        item_table, (0, ib * 2, st // 2, st % 2, 0, 0, 0), (2, 2, 1, 1, 4, 8, 128)
    ).reshape(2, 2, 4, 8, 128)
    picked = jnp.where(core == 0, picked, picked[::-1])
    item_rows = picked.transpose(1, 2, 0, 3, 4).reshape(128, 128)
    user_rows = lax.dynamic_slice_in_dim(user_factor, ub * 128, 128, 0)
    col = jnp.arange(128, dtype=jnp.int32)
    true_p = ((col % 64) // 4) * 8 + ((col // 64) ^ core) * 4 + col % 4
    mix = (col[:, None] == true_p[None, :])
    user_perm = jnp.dot(user_rows, mix.astype(BF), preferred_element_type=F32).astype(BF)

    g_core, g_user, g_item, g_ctx = tile_terms(
        core_half, user_perm, item_rows, ctx_rows, observed[0]
    )

    send_core = g_core.reshape(2, 4, 4, 4, 2, CORE_ROWS, 128).transpose(0, 1, 3, 4, 2, 5, 6)
    places = jnp.arange(2048, dtype=jnp.int32)
    picker = (places[:, None] == spot[None, :]).astype(F32)
    send_ctx = jnp.dot(
        picker, g_ctx, precision=lax.Precision.HIGHEST, preferred_element_type=F32
    ).reshape(2, 4, 4, 2, 4, CTX_ROWS, 128)
    send_item = jnp.dot(
        (places[:, None] == item_spot[None, :]).astype(F32),
        g_item, precision=lax.Precision.HIGHEST, preferred_element_type=F32,
    ).reshape(2, 4, 4, 2, 4, ITEM_ROWS, 128)
    send = jnp.concatenate([send_core, send_ctx, send_item], axis=5)
    total = reduce_all(send[0], send[1].astype(BF)) * scale

    g_user = dot_nt(g_user, mix.astype(F32), precision=lax.Precision.HIGHEST)
    x_here = (jnp.arange(4) == ub)[:, None, None, None]
    send_user = jnp.where(x_here, g_user.reshape(1, 2, 64, 128), 0.0).astype(BF)
    got_user = lax.all_to_all(send_user.reshape(8, 64, 128), ("x", "zl"), 0, 0, tiled=True)
    user_grad = jnp.sum(got_user.astype(F32), axis=0) * scale
    return (
        total[:CORE_ROWS],
        user_grad,
        total[CORE_ROWS + CTX_ROWS :],
        total[CORE_ROWS : CORE_ROWS + CTX_ROWS],
    )


def solution(mesh):
    fine = Mesh(mesh.devices.reshape(4, 4, 2, 4, 2), ALL)
    user, item = ("y", "zh", "core"), ("x", "zl")
    return jax.shard_map(
        local,
        mesh=fine,
        in_specs=(
            P(ALL, None, None, None),
            P(ALL),
            P(ALL),
            P(ALL),
            P(ALL, None),
            P(ALL, None),
            P(user, None),
            P(item, None),
            P(ALL, None),
        ),
        out_specs=(P(ALL, None),) * 4,
        check_vma=False,
    )
```

time: 2380 us -> 197 us (0.08)
  the two profiles are of different devices: /device:TPU:0 before, /device:TPU:8 now
where the time goes in v1:
time: 197 us; the launch traced here: 196 us
  blocking collectives  55 us (28%)
  waiting for transfers between devices  45.4 us (23%)
  matrix products  37 us (19%)
  other arithmetic  22.7 us (12%)
  starting transfers between devices  17 us (9%)
  local copies, waits for them, and re-layouts  15.8 us (8%)
  between operations  2.91 us (1%)
    all_to_all x1, blocking collectives, gather_all(): lax.all_to_all(jnp.broadcast_to(one[None], (32,) + one.shape), BIG, 0, 0,...  38.4 us
    all_to_all x1, waiting for transfers between devices, reduce_all(): lax.all_to_all(both.reshape(32, 4, ROWS, 128), BIG, 0, 0, tiled=True)  27.3 us
    all_to_all x1, blocking collectives, gather_all(): lax.all_to_all(jnp.broadcast_to(block[None], (4,) + block.shape), 'zh', 0...  16.6 us
    dot_general x1, matrix products, tile_terms(): predicted = jnp.dot(user_rows, second_flat, preferred_element_type=F32)  16.3 us
    dot_general x3, matrix products, dot_nt(): lax.dot_general(left, right, (((1,), (1,)), ((), ())), precision=precisio...  11.6 us
    all_to_all x1, waiting for transfers between devices, reduce_all(): last = lax.all_to_all(some, 'zh', 0, 0, tiled=True)  7.87 us
    all_to_all x1, starting transfers between devices, local(): lax.all_to_all(send_user.reshape(8, 64, 128), ('x', 'zl'), 0, 0, tiled=True)  6.52 us
    all_to_all x1, starting transfers between devices, reduce_all(): lax.all_to_all(both.reshape(32, 4, ROWS, 128), BIG, 0, 0, tiled=True)  6.52 us
  transfers between devices with their start and end apart: 5, of which 4 were waited for; matrix products, arithmetic and copies ran while one was open for 9% of the time, Pallas kernels for 0%

profile of v1, /device:TPU:8, one launch (start us, length us, event | category | flops | bytes accessed | tf_op | source)
XLA Modules:
  0.0 195.8 jit_solution(10313067505471694689)
XLA Ops:
  2.8 16.6 %all_to_all.25 = bf16[4,80,128]{2,1,0:T(8,128)(2,1)S(1)} all-to-all(bf16[4,80,128]{2,1,0:T(8,128)(2,1)S(1)} %broadcast_in_dim.57), channel_id=1, replica_groups=mesh['y'=4,'zh'=4,'core'=2,'x'=4,'zl'=2] {'zh'}, dimensions={0} | all-to-all | bytes 163840 | tf_op jit(solution)/shard_map/all_to_all | solution.py:31
  20.0 38.4 %all_to_all.26 = bf16[32,4,80,128]{3,2,1,0:T(8,128)(2,1)S(1)} all-to-all(bf16[32,4,80,128]{3,2,1,0:T(8,128)(2,1)S(1)} %broadcast_in_dim.58), channel_id=1, replica_groups=mesh['y'=4,'zh'=4,'core'=2,'x'=4,'zl'=2] {'y','x','zl'}, dimensions={0} | all-to-all | bytes 5242880 | tf_op jit(solution)/shard_map/all_to_all | solution.py:34
  60.4 6.5 %convert.9 = f32[16,8,128,128]{3,2,1,0:T(8,128)} convert(bf16[16,8,128,128]{3,2,1,0:T(8,128)(2,1)} %bitcast.111) | non-fusion elementwise | flops 2097152 | bytes 12582912
  68.2 1.8 fusion.4
  70.7 2.9 %copy.28 = bf16[2,4,4,4,2,64,128]{6,5,4,3,2,1,0:T(8,128)(2,1)} copy(bf16[2,4,4,4,2,64,128]{6,5,2,4,3,1,0:T(8,128)(2,1)S(1)} %fusion.4) | data formatting | bytes 8388608 | tf_op jit(solution)/shard_map/transpose | solution.py:90
  74.3 3.5 %convolution_convert_fusion.1 = bf16[16384,128]{1,0:T(8,128)(2,1)S(1)} fusion(bf16[16384,128]{1,0:T(8,128)(2,1)} %bitcast.98, bf16[128,128]{1,0:T(8,128)(2,1)S(1)} %gather_fusion, pred[128]{0:T(512)(128)(4,1)S(1)} %get-tuple-element.4), kind=kOutput, calls=%fused_computation.4 | convolution fusion | flops 538984448 | bytes 8421504 | tf_op jit(solution)/shard_map/dot_general | solution.py:17
  79.1 1.9 copy-done.3
  81.0 16.3 %fusion = bf16[128,16384]{1,0:T(8,128)(2,1)S(1)} fusion(bf16[128,128]{1,0:T(8,128)(2,1)S(1)} %convolution_convert_fusion.4, f32[16,8,128,128]{3,2,1,0:T(8,128)} %convert.9, bf16[16,8,128,128]{3,2,1,0:T(8,128)(2,1)S(1)} %bitcast.108), kind=kOutput, calls=%fused_computation.2 | convolution fusion | flops 541065216 | bytes 16809984 | tf_op jit(solution)/shard_map/dot_general | solution.py:58
  97.3 1.3 fusion.11
  101.8 1.3 convolution_convert_fusion.2
  104.0 1.4 fusion.39
  105.4 1.3 convolution_bitcast_fusion
  107.9 5.3 %pad_maximum_fusion = f32[2,4,4,2,4,80,128]{6,5,3,2,4,1,0:T(8,128)} fusion(f32[2,4,4,2,4,64,128]{6,5,3,2,4,1,0:T(8,128)S(1)} %convolution_bitcast_fusion, f32[2,4,4,2,4,8,128]{6,5,4,3,2,1,0:T(8,128)S(1)} %bitcast.112, f32[2,4,4,2,4,8,128]{6,5,4,3,2,1,0:T(8,128)S(1)} %bitcast.113), kind=kLoop, calls=%fused_computation.5 | loop fusion | flops 5242880 | bytes 20971520 | tf_op jit(solution)/shard_map/concatenate | solution.py:127
  113.2 2.9 %fusion.10 = bf16[4,4,2,4,80,128]{5,4,2,1,3,0:T(8,128)(2,1)S(1)} fusion(f32[2,4,4,2,4,80,128]{6,5,3,2,4,1,0:T(8,128)} %pad_maximum_fusion), kind=kLoop, calls=%fused_computation.23 | loop fusion | bytes 5242880 | tf_op jit(solution)/shard_map/convert_element_type | solution.py:128
  116.7 4.5 %collective-permute-done.1 = bf16[4,4,2,4,80,128]{5,4,2,1,3,0:T(8,128)(2,1)S(1)} collective-permute-done((bf16[4,4,2,4,80,128]{5,4,2,1,3,0:T(8,128)(2,1)S(1)}, bf16[4,4,2,4,80,128]{5,4,2,1,3,0:T(8,128)(2,1)S(1)}, u32[]{:S(2)}, u32[]{:S(2)}) %collective-permute-start.1) | collective-permute-done | bytes 2621472 | tf_op jit(solution)/shard_map/ppermute | solution.py:27
  121.2 3.4 %fusion.2 = bf16[4,4,2,4,80,128]{5,4,2,1,3,0:T(8,128)(2,1)S(1)} fusion(f32[2,4,4,2,4,80,128]{6,5,3,2,4,1,0:T(8,128)} %pad_maximum_fusion, bf16[4,4,2,4,80,128]{5,4,2,1,3,0:T(8,128)(2,1)S(1)} %collective-permute-done.1), kind=kLoop, calls=%fused_computation.9 | loop fusion | flops 3932160 | bytes 10485760 | tf_op jit(solution)/shard_map/convert_element_type | solution.py:41
  124.6 1.9 copy.32
  126.5 6.5 %all-to-all-start.2 = ((bf16[32,4,80,128]{3,2,1,0:T(8,128)(2,1)}), bf16[32,4,80,128]{3,2,1,0:T(8,128)(2,1)S(1)}, u32[]{:S(2)}, u32[]{:S(2)}) async-start(bf16[32,4,80,128]{3,2,1,0:T(8,128)(2,1)} %bitcast.110), calls=%async_computation.2 | async-start | bytes 5242880 | tf_op jit(solution)/shard_map/all_to_all | solution.py:42
  133.2 7.9 %fusion.5 = f32[128,128]{1,0:T(8,128)S(1)} fusion(bf16[128,16384]{1,0:T(8,128)(2,1)} %copy-done.4, bf16[16,8,128,128]{3,2,1,0:T(8,128)(2,1)} %bitcast.109), kind=kOutput, calls=%fused_computation.15 | convolution fusion | flops 536870912 | bytes 8454144 | tf_op jit(solution)/shard_map/dot_general | solution.py:17
  142.1 27.3 %all-to-all-done.2 = bf16[32,4,80,128]{3,2,1,0:T(8,128)(2,1)S(1)} async-done(((bf16[32,4,80,128]{3,2,1,0:T(8,128)(2,1)}), bf16[32,4,80,128]{3,2,1,0:T(8,128)(2,1)S(1)}, u32[]{:S(2)}, u32[]{:S(2)}) %all-to-all-start.2) | async-done | bytes 2621472 | tf_op jit(solution)/shard_map/all_to_all | solution.py:42
  169.5 6.5 %all-to-all-start.4 = ((bf16[8,64,128]{2,1,0:T(8,128)(2,1)}), bf16[8,64,128]{2,1,0:T(8,128)(2,1)S(1)}, u32[]{:S(2)}, u32[]{:S(2)}) async-start(bf16[8,64,128]{2,1,0:T(8,128)(2,1)} %fusion.16), calls=%async_computation.4 | async-start | bytes 262144 | tf_op jit(solution)/shard_map/all_to_all | solution.py:133
  177.0 5.7 %all-to-all-done.4 = bf16[8,64,128]{2,1,0:T(8,128)(2,1)S(1)} async-done(((bf16[8,64,128]{2,1,0:T(8,128)(2,1)}), bf16[8,64,128]{2,1,0:T(8,128)(2,1)S(1)}, u32[]{:S(2)}, u32[]{:S(2)}) %all-to-all-start.4) | async-done | bytes 131104 | tf_op jit(solution)/shard_map/all_to_all | solution.py:133
  182.7 3.3 %all-to-all-start.3 = ((f32[4,80,128]{2,1,0:T(8,128)}), f32[4,80,128]{2,1,0:T(8,128)S(1)}, u32[]{:S(2)}, u32[]{:S(2)}) async-start(f32[4,80,128]{2,1,0:T(8,128)} %convert_reduce_fusion), calls=%async_computation.3 | async-start | bytes 327680 | tf_op jit(solution)/shard_map/all_to_all | solution.py:44
  186.7 7.9 %all-to-all-done.3 = f32[4,80,128]{2,1,0:T(8,128)S(1)} async-done(((f32[4,80,128]{2,1,0:T(8,128)}), f32[4,80,128]{2,1,0:T(8,128)S(1)}, u32[]{:S(2)}, u32[]{:S(2)}) %all-to-all-start.3) | async-done | bytes 163872 | tf_op jit(solution)/shard_map/all_to_all | solution.py:44
  (46 shorter events, 16.6 us)
Async XLA Ops:
  0.6 66.4 %copy-start = (bf16[512,128]{1,0:T(8,128)(2,1)S(1)}, bf16[512,128]{1,0:T(8,128)(2,1)}, u32[]{:S(2)}) copy-start(bf16[512,128]{1,0:T(8,128)(2,1)} %param.15) | copy-start | bytes 393220
  58.4 8.8 %collective-permute-start = (bf16[4,4,2,4,80,128]{5,4,3,2,1,0:T(8,128)(2,1)S(1)}, bf16[4,4,2,4,80,128]{5,4,3,2,1,0:T(8,128)(2,1)}, u32[]{:S(2)}, u32[]{:S(2)}) collective-permute-start(bf16[4,4,2,4,80,128]{5,4,3,2,1,0:T(8,128)(2,1)S(1)} %bitcast.102), channel_id=1, source_target_pairs={{0,8},{8,0},{1,9},{9,1},{2,10},{10,2},{3,11},{11,3},{4,12},{12,4},... | collective-permute-start | bytes 7864328 | tf_op jit(solution)/shard_map/ppermute | solution.py:27
  60.4 6.6 %copy-start.5 = (s32[1,128]{1,0:T(1,128)S(1)}, s32[1,128]{1,0:T(1,128)}, u32[]{:S(2)}) copy-start(s32[1,128]{1,0:T(1,128)} %param.13) | copy-start | bytes 1540
  79.1 1.9 copy-start.3
  97.3 2.0 %copy-start.4 = (bf16[128,16384]{1,0:T(8,128)(2,1)}, bf16[128,16384]{1,0:T(8,128)(2,1)S(1)}, u32[]{:S(2)}) copy-start(bf16[128,16384]{1,0:T(8,128)(2,1)S(1)} %fusion) | copy-start | bytes 12582916
  101.8 2.2 %copy-start.2 = (bf16[2,4,4,4,2,64,128]{6,5,4,3,2,1,0:T(8,128)(2,1)S(1)}, bf16[2,4,4,4,2,64,128]{6,5,4,3,2,1,0:T(8,128)(2,1)}, u32[]{:S(2)}) copy-start(bf16[2,4,4,4,2,64,128]{6,5,4,3,2,1,0:T(8,128)(2,1)} %copy.28) | copy-start | bytes 12582916
  116.1 5.1 %collective-permute-start.1 = (bf16[4,4,2,4,80,128]{5,4,2,1,3,0:T(8,128)(2,1)S(1)}, bf16[4,4,2,4,80,128]{5,4,2,1,3,0:T(8,128)(2,1)S(1)}, u32[]{:S(2)}, u32[]{:S(2)}) collective-permute-start(bf16[4,4,2,4,80,128]{5,4,2,1,3,0:T(8,128)(2,1)S(1)} %fusion.10), channel_id=1, source_target_pairs={{0,8},{8,0},{1,9},{9,1},{2,10},{10,2},{3,11},{11,3},{4,12},{12,4},... | collective-permute-start | bytes 7864328 | tf_op jit(solution)/shard_map/ppermute | solution.py:27
  126.5 42.9 %all-to-all-start.2 = ((bf16[32,4,80,128]{3,2,1,0:T(8,128)(2,1)}), bf16[32,4,80,128]{3,2,1,0:T(8,128)(2,1)S(1)}, u32[]{:S(2)}, u32[]{:S(2)}) async-start(bf16[32,4,80,128]{3,2,1,0:T(8,128)(2,1)} %bitcast.110), calls=%async_computation.2 | async-start | bytes 5242880 | tf_op jit(solution)/shard_map/all_to_all | solution.py:42
  133.2 62.6 %copy-start.1 = (bf16[512,128]{1,0:T(8,128)(2,1)S(1)}, bf16[512,128]{1,0:T(8,128)(2,1)}, u32[]{:S(2)}) copy-start(bf16[512,128]{1,0:T(8,128)(2,1)} %param.15) | copy-start | bytes 393220
  169.5 13.2 %all-to-all-start.4 = ((bf16[8,64,128]{2,1,0:T(8,128)(2,1)}), bf16[8,64,128]{2,1,0:T(8,128)(2,1)S(1)}, u32[]{:S(2)}, u32[]{:S(2)}) async-start(bf16[8,64,128]{2,1,0:T(8,128)(2,1)} %fusion.16), calls=%async_computation.4 | async-start | bytes 262144 | tf_op jit(solution)/shard_map/all_to_all | solution.py:133
  182.7 11.9 %all-to-all-start.3 = ((f32[4,80,128]{2,1,0:T(8,128)}), f32[4,80,128]{2,1,0:T(8,128)S(1)}, u32[]{:S(2)}, u32[]{:S(2)}) async-start(f32[4,80,128]{2,1,0:T(8,128)} %convert_reduce_fusion), calls=%async_computation.3 | async-start | bytes 327680 | tf_op jit(solution)/shard_map/all_to_all | solution.py:44

commit v2 on v1

v2 whole, which is shorter than its diff:
```python
import math

import jax
import jax.numpy as jnp
from jax import lax
from jax.sharding import Mesh, PartitionSpec as P

BF = jnp.bfloat16
F32 = jnp.float32
ALL = ("y", "zh", "core", "x", "zl")
BIG = ("y", "x", "zl")
CORE_ROWS, CTX_ROWS, ITEM_ROWS = 64, 8, 8
ROWS = CORE_ROWS + CTX_ROWS + ITEM_ROWS


def dot_nt(left, right, precision=None):
    return lax.dot_general(
        left, right, (((1,), (1,)), ((), ())), precision=precision, preferred_element_type=F32
    )


def dot_tn(left, right):
    return lax.dot_general(left, right, (((0,), (0,)), ((), ())), preferred_element_type=F32)


def swap(value):
    return lax.ppermute(value, "core", [(0, 1), (1, 0)])


def gather_all(block, beside):
    one = lax.all_to_all(
        jnp.broadcast_to(block[None], (4,) + block.shape), "zh", 0, 0, tiled=True
    ).reshape(4 * ROWS, 128)
    one, beside = lax.optimization_barrier((one, beside))
    beside = beside.reshape(128, 16384)
    own = lax.all_to_all(jnp.broadcast_to(one[None], (32,) + one.shape), BIG, 0, 0, tiled=True)
    own, beside = lax.optimization_barrier((own, beside))
    own = own.reshape(4, 4, 2, 4, ROWS, 128)
    return own, swap(own), beside


def local(
    observed,
    user_block,
    item_block,
    stratum,
    context_ids,
    core_tensor,
    user_factor,
    item_factor,
    context_factor,
):
    y, zh, core, x, zl = (lax.axis_index(name) for name in ALL)
    scale = 1.0 / math.sqrt(128 * 128 * 128)
    ub, ib, st, ids = user_block[0], item_block[0], stratum[0], context_ids[0]
    mine = (y * 4 + zh) * 2 + core
    item_own = lax.dynamic_slice_in_dim(item_factor, mine * ITEM_ROWS, ITEM_ROWS, 0)
    block = jnp.concatenate([core_tensor.astype(BF), context_factor, item_own], axis=0)
    own, other, seen = gather_all(block, observed[0])
    both = jnp.stack([own, other])

    core_half = both[..., :CORE_ROWS, :].transpose(0, 1, 2, 4, 3, 5, 6).reshape(16384, 128)
    def spot_of(row):
        j, d = row & 7, row >> 3
        d_zl, d_x, d_c, d_zh, d_y = d & 1, (d >> 1) & 3, (d >> 3) & 1, (d >> 4) & 3, d >> 6
        place = ((((d_c ^ core) * 4 + d_y) * 4 + d_x) * 2 + d_zl) * 4 + d_zh
        return place * 8 + j

    spot = spot_of(ids)
    item_spot = spot_of((st * 2 + ib) * 128 + jnp.arange(128, dtype=jnp.int32))
    ctx_table = both[..., CORE_ROWS : CORE_ROWS + CTX_ROWS, :].reshape(2048, 128)
    ctx_rows = jnp.take(ctx_table, spot, axis=0)
    item_table = both[..., CORE_ROWS + CTX_ROWS :, :]
    picked = lax.dynamic_slice(
        item_table, (0, ib * 2, st // 2, st % 2, 0, 0, 0), (2, 2, 1, 1, 4, 8, 128)
    ).reshape(2, 2, 4, 8, 128)
    picked = jnp.where(core == 0, picked, picked[::-1])
    item_rows = picked.transpose(1, 2, 0, 3, 4).reshape(128, 128)
    user_rows = lax.dynamic_slice_in_dim(user_factor, ub * 128, 128, 0)
    col = jnp.arange(128, dtype=jnp.int32)
    true_p = ((col >> 4) & 3) * 32 + (col & 3) * 8 + ((col >> 6) ^ core) * 4 + ((col >> 2) & 3)
    mix = (col[:, None] == true_p[None, :])
    user_perm = jnp.dot(user_rows, mix.astype(BF), preferred_element_type=F32).astype(BF)

    first = dot_nt(core_half, ctx_rows).astype(BF).reshape(128, 128, 128)
    second = jnp.einsum("pqc,bq->pbc", first, item_rows, preferred_element_type=F32)
    second = second.astype(BF).reshape(128, 16384)
    predicted = jnp.dot(user_perm, second, preferred_element_type=F32)
    residual = (predicted - seen.astype(F32)).astype(BF)
    g_user = dot_nt(residual, second)
    back = dot_tn(user_perm, residual).astype(BF).reshape(128, 128, 128)
    folded = jnp.einsum("pbc,bq->pqc", back, item_rows, preferred_element_type=F32)
    folded = folded.astype(BF).reshape(16384, 128)
    g_other = jnp.dot(folded[8192:], ctx_rows, preferred_element_type=F32).astype(BF)
    got_core = swap(g_other)
    g_item = jnp.einsum("pbc,pqc->bq", back, first, preferred_element_type=F32)
    g_ctx = dot_tn(folded, core_half)

    places = jnp.arange(2048, dtype=jnp.int32)
    send_ctx = jnp.dot(
        (places[:, None] == spot[None, :]).astype(F32),
        g_ctx, precision=lax.Precision.HIGHEST, preferred_element_type=F32,
    )
    send_item = jnp.dot(
        (places[:, None] == item_spot[None, :]).astype(F32),
        g_item, precision=lax.Precision.HIGHEST, preferred_element_type=F32,
    )
    send = jnp.stack([send_ctx, send_item]).reshape(2, 2, 1024, 128)
    small = (send[:, 0] + swap(send[:, 1].astype(BF)).astype(F32)).astype(BF)
    small = small.reshape(2, 32, 4, 8, 128).transpose(1, 2, 0, 3, 4).reshape(32, 4, 16, 128)
    g_own = jnp.dot(folded[:8192], ctx_rows, preferred_element_type=F32)
    core_sum = (g_own + got_core.astype(F32)).astype(BF)
    core_sum = core_sum.reshape(4, 4, 4, 2, CORE_ROWS, 128).transpose(0, 1, 3, 2, 4, 5)
    both = jnp.concatenate([core_sum.reshape(32, 4, CORE_ROWS, 128), small], axis=2)
    parts = lax.all_to_all(both.reshape(32, 4 * ROWS, 128), BIG, 0, 0, tiled=True)

    g_user = dot_nt(g_user, mix.astype(F32), precision=lax.Precision.HIGHEST)
    x_here = (jnp.arange(4) == ub)[:, None, None, None]
    send_user = jnp.where(x_here, g_user.reshape(1, 2, 64, 128), 0.0).astype(BF)
    got_user = lax.all_to_all(send_user.reshape(8, 64, 128), ("x", "zl"), 0, 0, tiled=True)
    user_grad = jnp.sum(got_user.astype(F32), axis=0) * scale

    some = jnp.sum(parts.astype(F32), axis=0).reshape(4, ROWS, 128)
    last = lax.all_to_all(some, "zh", 0, 0, tiled=True)
    total = jnp.sum(last, axis=0) * scale
    return (
        total[:CORE_ROWS],
        user_grad,
        total[CORE_ROWS + CTX_ROWS :],
        total[CORE_ROWS : CORE_ROWS + CTX_ROWS],
    )


def solution(mesh):
    fine = Mesh(mesh.devices.reshape(4, 4, 2, 4, 2), ALL)
    user, item = ("y", "zh", "core"), ("x", "zl")
    return jax.shard_map(
        local,
        mesh=fine,
        in_specs=(
            P(ALL, None, None, None),
            P(ALL),
            P(ALL),
            P(ALL),
            P(ALL, None),
            P(ALL, None),
            P(user, None),
            P(item, None),
            P(ALL, None),
        ),
        out_specs=(P(ALL, None),) * 4,
        check_vma=False,
    )
```

time: 197 us -> 167 us (0.85)
  blocking collectives: 55 us -> 16.6 us
  waiting for transfers between devices: 45.4 us -> 66 us
  other arithmetic: 22.7 us -> 9.47 us
  matrix products: 37 us -> 24.2 us
  starting transfers between devices: 17 us -> 26.3 us
  local copies, waits for them, and re-layouts: 15.8 us -> 20.2 us
    all_to_all x1 -> x0, blocking collectives: 38.4 us -> none  [gather_all(): lax.all_to_all(jnp.broadcast_to(one[None], (32,) + one.shape), BIG, 0, 0,...]
    all_to_all x2 -> x3, waiting for transfers between devices: 35.2 us -> 55.8 us  [the longest x1 24.5 us: local(): lax.all_to_all(both.reshape(32, 4 * ROWS, 128), BIG, 0, 0, tiled=True)]
    dot_general x6 -> x7, matrix products: 21.9 us -> 9.3 us  [the longest x1 3.36 us: local(): predicted = jnp.dot(user_perm, second, preferred_element_type=F32)]
    all_to_all x2 -> x3, starting transfers between devices: 9.86 us -> 18.1 us  [the longest x1 7.99 us: gather_all(): lax.all_to_all(jnp.broadcast_to(one[None], (32,) + one.shape), BIG, 0, 0,...]
    unnamed x13 -> x16, local copies, waits for them, and re-layouts: 4.78 us -> 11.5 us
    unnamed x1 -> x0, other arithmetic: 6.52 us -> none
    convert_element_type x2 -> x0, local copies, waits for them, and re-layouts: 4.8 us -> none  [the longest x1 2.89 us: local(): total = reduce_all(send[0], send[1].astype(BF)) * scale]
    concatenate x1, other arithmetic: 5.28 us -> 1.78 us  [local(): jnp.concatenate([core_sum.reshape(32, 4, CORE_ROWS, 128), small], axis=2)]
  transfers between devices with their start and end apart: 5 -> 7, of which waited for: 4 -> 6; matrix products, arithmetic and copies ran while one was open for 9% -> 14% of each run, Pallas kernels for 0% -> 0%
where the time goes in v2:
time: 167 us; the launch traced here: 166 us
  waiting for transfers between devices  66 us (40%)
  starting transfers between devices  26.3 us (16%)
  matrix products  24.2 us (14%)
  local copies, waits for them, and re-layouts  20.2 us (12%)
  blocking collectives  16.6 us (10%)
  other arithmetic  9.47 us (6%)
  between operations  2.96 us (2%)
    all_to_all x1, waiting for transfers between devices, local(): lax.all_to_all(both.reshape(32, 4 * ROWS, 128), BIG, 0, 0, tiled=True)  24.5 us
    all_to_all x1, waiting for transfers between devices, gather_all(): lax.all_to_all(jnp.broadcast_to(one[None], (32,) + one.shape), BIG, 0, 0,...  23.3 us
    all_to_all x1, blocking collectives, gather_all(): lax.all_to_all(jnp.broadcast_to(block[None], (4,) + block.shape), 'zh', 0...  16.6 us
    dot_general x3, matrix products, dot_nt(): lax.dot_general(left, right, (((1,), (1,)), ((), ())), precision=precisio...  11.6 us
    unnamed x16, local copies, waits for them, and re-layouts  11.5 us
    all_to_all x1, starting transfers between devices, gather_all(): lax.all_to_all(jnp.broadcast_to(one[None], (32,) + one.shape), BIG, 0, 0,...  7.99 us
    all_to_all x1, waiting for transfers between devices, local(): last = lax.all_to_all(some, 'zh', 0, 0, tiled=True)  7.88 us
    all_to_all x1, starting transfers between devices, local(): lax.all_to_all(send_user.reshape(8, 64, 128), ('x', 'zl'), 0, 0, tiled=True)  7.48 us
  transfers between devices with their start and end apart: 7, of which 6 were waited for; matrix products, arithmetic and copies ran while one was open for 14% of the time, Pallas kernels for 0%

profile of v2, /device:TPU:8, one launch (start us, length us, event | category | flops | bytes accessed | tf_op | source)
XLA Modules:
  0.0 165.8 jit_solution(10205167451514650952)
XLA Ops:
  2.8 16.6 %all_to_all.25 = bf16[4,80,128]{2,1,0:T(8,128)(2,1)S(1)} all-to-all(bf16[4,80,128]{2,1,0:T(8,128)(2,1)S(1)} %broadcast_in_dim.57), channel_id=1, replica_groups=mesh['y'=4,'zh'=4,'core'=2,'x'=4,'zl'=2] {'zh'}, dimensions={0} | all-to-all | bytes 163840 | tf_op jit(solution)/shard_map/all_to_all | solution.py:31
  19.4 2.1 %broadcast_in_dim.58 = bf16[32,320,128]{2,1,0:T(8,128)(2,1)} broadcast(bf16[320,128]{1,0:T(8,128)(2,1)S(1)} %bitcast.134), dimensions={1,2} | broadcast | bytes 2703360 | tf_op jit(solution)/shard_map/broadcast_in_dim | solution.py:36
  21.6 8.0 %all-to-all-start.1 = ((bf16[32,320,128]{2,1,0:T(8,128)(2,1)}), bf16[32,320,128]{2,1,0:T(8,128)(2,1)S(1)}, u32[]{:S(2)}, u32[]{:S(2)}) async-start(bf16[32,320,128]{2,1,0:T(8,128)(2,1)} %broadcast_in_dim.58), calls=%async_computation.1 | async-start | bytes 5242880 | tf_op jit(solution)/shard_map/all_to_all | solution.py:36
  29.6 7.7 %copy.50 = bf16[16,8,128,128]{3,1,2,0:T(8,128)(2,1)} copy(bf16[16,8,128,128]{3,2,1,0:T(8,128)(2,1)} %bitcast.130) | data formatting | bytes 8388608
  37.3 23.3 %all-to-all-done.1 = bf16[32,320,128]{2,1,0:T(8,128)(2,1)S(1)} async-done(((bf16[32,320,128]{2,1,0:T(8,128)(2,1)}), bf16[32,320,128]{2,1,0:T(8,128)(2,1)S(1)}, u32[]{:S(2)}, u32[]{:S(2)}) %all-to-all-start.1) | async-done | bytes 2621472 | tf_op jit(solution)/shard_map/all_to_all | solution.py:36
  62.8 2.8 %collective-permute-done = bf16[4,4,2,4,80,128]{5,4,3,2,1,0:T(8,128)(2,1)} collective-permute-done((bf16[4,4,2,4,80,128]{5,4,3,2,1,0:T(8,128)(2,1)S(1)}, bf16[4,4,2,4,80,128]{5,4,3,2,1,0:T(8,128)(2,1)}, u32[]{:S(2)}, u32[]{:S(2)}) %collective-permute-start) | collective-permute-done | bytes 2621472 | tf_op jit(solution)/shard_map/ppermute | solution.py:27
  66.7 1.8 %fusion.2 = bf16[2,4,4,4,2,64,128]{6,5,3,4,2,1,0:T(8,128)(2,1)S(1)} fusion(bf16[1,4,4,2,4,80,128]{6,5,4,3,2,1,0:T(8,128)(2,1)S(1)} %bitcast.114, bf16[1,4,4,2,4,80,128]{6,5,4,3,2,1,0:T(8,128)(2,1)} %bitcast.4), kind=kLoop, calls=%fused_computation.10 | loop fusion | flops 2097152 | bytes 9437184 | tf_op jit(solution)/shard_map/transpose | solution.py:62
  69.2 2.9 %copy.29 = bf16[2,4,4,4,2,64,128]{6,5,4,3,2,1,0:T(8,128)(2,1)} copy(bf16[2,4,4,4,2,64,128]{6,5,3,4,2,1,0:T(8,128)(2,1)S(1)} %fusion.2) | data formatting | bytes 8388608 | tf_op jit(solution)/shard_map/transpose | solution.py:62
  72.9 3.5 %convolution_convert_fusion.1 = bf16[16384,128]{1,0:T(8,128)(2,1)S(1)} fusion(bf16[16384,128]{1,0:T(8,128)(2,1)} %bitcast.106, bf16[128,128]{1,0:T(8,128)(2,1)S(1)} %gather_fusion, pred[128]{0:T(512)(128)(4,1)S(1)} %get-tuple-element.12), kind=kOutput, calls=%fused_computation.4 | convolution fusion | flops 538984448 | bytes 8421504 | tf_op jit(solution)/shard_map/dot_general | solution.py:17
  76.4 1.2 convolution_convert_fusion.4
  78.6 3.4 %fusion = bf16[128,16384]{1,0:T(8,128)(2,1)S(1)} fusion(bf16[128,128]{1,0:T(8,128)(2,1)S(1)} %convolution_convert_fusion.5, bf16[128,16384]{1,0:T(8,128)(2,1)S(1)} %bitcast.118, bf16[16,8,128,128]{3,2,1,0:T(8,128)(2,1)S(1)} %bitcast.119), kind=kOutput, calls=%fused_computation.2 | convolution fusion | flops 543162368 | bytes 12615680 | tf_op jit(solution)/shard_map/dot_general | solution.py:88
  81.9 1.3 fusion.8
  83.9 1.2 copy.39
  85.1 1.3 convolution_convert_fusion.3
  89.2 1.3 fusion.43
  93.2 1.8 %collective-permute-done.2 = bf16[2,1024,128]{2,1,0:T(8,128)(2,1)S(1)} collective-permute-done((bf16[2,1024,128]{2,1,0:T(8,128)(2,1)S(1)}, bf16[2,1024,128]{2,1,0:T(8,128)(2,1)S(1)}, u32[]{:S(2)}, u32[]{:S(2)}) %collective-permute-start.2) | collective-permute-done | bytes 524320 | tf_op jit(solution)/shard_map/ppermute | solution.py:27
  96.3 1.8 %pad_maximum_fusion = bf16[32,4,80,128]{3,2,1,0:T(8,128)(2,1)} fusion(bf16[32,4,16,128]{3,2,1,0:T(8,128)(2,1)S(1)} %bitcast.131, bf16[32,4,64,128]{3,2,1,0:T(8,128)(2,1)S(1)} %bitcast.129), kind=kLoop, calls=%fused_computation.20 | loop fusion | flops 5242880 | bytes 5242880 | tf_op jit(solution)/shard_map/concatenate | solution.py:114
  98.0 6.8 %all-to-all-start.2 = ((bf16[32,320,128]{2,1,0:T(8,128)(2,1)}), bf16[32,320,128]{2,1,0:T(8,128)(2,1)S(1)}, u32[]{:S(2)}, u32[]{:S(2)}) async-start(bf16[32,320,128]{2,1,0:T(8,128)(2,1)} %bitcast.122), calls=%async_computation.2 | async-start | bytes 5242880 | tf_op jit(solution)/shard_map/all_to_all | solution.py:115
  105.0 7.9 %fusion.3 = f32[128,128]{1,0:T(8,128)S(1)} fusion(bf16[128,16384]{1,0:T(8,128)(2,1)} %copy-done.5, bf16[16,8,128,128]{3,2,1,0:T(8,128)(2,1)} %bitcast.120), kind=kOutput, calls=%fused_computation.11 | convolution fusion | flops 536870912 | bytes 8454144 | tf_op jit(solution)/shard_map/dot_general | solution.py:17
  113.9 24.5 %all-to-all-done.2 = bf16[32,320,128]{2,1,0:T(8,128)(2,1)S(1)} async-done(((bf16[32,320,128]{2,1,0:T(8,128)(2,1)}), bf16[32,320,128]{2,1,0:T(8,128)(2,1)S(1)}, u32[]{:S(2)}, u32[]{:S(2)}) %all-to-all-start.2) | async-done | bytes 2621472 | tf_op jit(solution)/shard_map/all_to_all | solution.py:115
  138.5 7.5 %all-to-all-start.4 = ((bf16[8,64,128]{2,1,0:T(8,128)(2,1)}), bf16[8,64,128]{2,1,0:T(8,128)(2,1)S(1)}, u32[]{:S(2)}, u32[]{:S(2)}) async-start(bf16[8,64,128]{2,1,0:T(8,128)(2,1)} %fusion.19), calls=%async_computation.4 | async-start | bytes 262144 | tf_op jit(solution)/shard_map/all_to_all | solution.py:120
  147.0 5.7 %all-to-all-done.4 = bf16[8,64,128]{2,1,0:T(8,128)(2,1)S(1)} async-done(((bf16[8,64,128]{2,1,0:T(8,128)(2,1)}), bf16[8,64,128]{2,1,0:T(8,128)(2,1)S(1)}, u32[]{:S(2)}, u32[]{:S(2)}) %all-to-all-start.4) | async-done | bytes 131104 | tf_op jit(solution)/shard_map/all_to_all | solution.py:120
  152.7 3.3 %all-to-all-start.3 = ((f32[4,80,128]{2,1,0:T(8,128)}), f32[4,80,128]{2,1,0:T(8,128)S(1)}, u32[]{:S(2)}, u32[]{:S(2)}) async-start(f32[4,80,128]{2,1,0:T(8,128)} %bitcast.39), calls=%async_computation.3 | async-start | bytes 327680 | tf_op jit(solution)/shard_map/all_to_all | solution.py:124
  156.7 7.9 %all-to-all-done.3 = f32[4,80,128]{2,1,0:T(8,128)S(1)} async-done(((f32[4,80,128]{2,1,0:T(8,128)}), f32[4,80,128]{2,1,0:T(8,128)S(1)}, u32[]{:S(2)}, u32[]{:S(2)}) %all-to-all-start.3) | async-done | bytes 163872 | tf_op jit(solution)/shard_map/all_to_all | solution.py:124
  (55 shorter events, 17.2 us)
Async XLA Ops:
  0.6 62.1 %copy-start = (bf16[512,128]{1,0:T(8,128)(2,1)S(1)}, bf16[512,128]{1,0:T(8,128)(2,1)}, u32[]{:S(2)}) copy-start(bf16[512,128]{1,0:T(8,128)(2,1)} %param.15) | copy-start | bytes 393220
  21.6 39.0 %all-to-all-start.1 = ((bf16[32,320,128]{2,1,0:T(8,128)(2,1)}), bf16[32,320,128]{2,1,0:T(8,128)(2,1)S(1)}, u32[]{:S(2)}, u32[]{:S(2)}) async-start(bf16[32,320,128]{2,1,0:T(8,128)(2,1)} %broadcast_in_dim.58), calls=%async_computation.1 | async-start | bytes 5242880 | tf_op jit(solution)/shard_map/all_to_all | solution.py:36
  29.6 33.1 %copy-start.6 = (s32[1,128]{1,0:T(1,128)S(1)}, s32[1,128]{1,0:T(1,128)}, u32[]{:S(2)}) copy-start(s32[1,128]{1,0:T(1,128)} %param.13) | copy-start | bytes 1540
  60.6 5.0 %collective-permute-start = (bf16[4,4,2,4,80,128]{5,4,3,2,1,0:T(8,128)(2,1)S(1)}, bf16[4,4,2,4,80,128]{5,4,3,2,1,0:T(8,128)(2,1)}, u32[]{:S(2)}, u32[]{:S(2)}) collective-permute-start(bf16[4,4,2,4,80,128]{5,4,3,2,1,0:T(8,128)(2,1)S(1)} %bitcast.112), channel_id=1, source_target_pairs={{0,8},{8,0},{1,9},{9,1},{2,10},{10,2},{3,11},{11,3},{4,12},{12,4},... | collective-permute-start | bytes 7864328 | tf_op jit(solution)/shard_map/ppermute | solution.py:27
  76.4 2.2 %copy-start.3 = (bf16[16,8,128,128]{3,1,2,0:T(8,128)(2,1)S(1)}, bf16[16,8,128,128]{3,1,2,0:T(8,128)(2,1)}, u32[]{:S(2)}) copy-start(bf16[16,8,128,128]{3,1,2,0:T(8,128)(2,1)} %copy.50) | copy-start | bytes 12582916
  77.6 4.3 %copy-start.4 = (bf16[128,128,128]{2,0,1:T(8,128)(2,1)}, bf16[128,128,128]{2,0,1:T(8,128)(2,1)S(1)}, u32[]{:S(2)}) copy-start(bf16[128,128,128]{2,0,1:T(8,128)(2,1)S(1)} %convolution_convert_fusion.4) | copy-start | bytes 12582916
  81.9 2.0 %copy-start.5 = (bf16[128,16384]{1,0:T(8,128)(2,1)}, bf16[128,16384]{1,0:T(8,128)(2,1)S(1)}, u32[]{:S(2)}) copy-start(bf16[128,16384]{1,0:T(8,128)(2,1)S(1)} %fusion) | copy-start | bytes 12582916
  87.0 2.2 %copy-start.2 = (bf16[2,4,4,4,2,64,128]{6,5,4,3,2,1,0:T(8,128)(2,1)S(1)}, bf16[2,4,4,4,2,64,128]{6,5,4,3,2,1,0:T(8,128)(2,1)}, u32[]{:S(2)}) copy-start(bf16[2,4,4,4,2,64,128]{6,5,4,3,2,1,0:T(8,128)(2,1)} %copy.29) | copy-start | bytes 12582916
  87.7 7.5 %collective-permute-start.1 = (bf16[8192,128]{1,0:T(8,128)(2,1)S(1)}, bf16[8192,128]{1,0:T(8,128)(2,1)S(1)}, u32[]{:S(2)}, u32[]{:S(2)}) collective-permute-start(bf16[8192,128]{1,0:T(8,128)(2,1)S(1)} %convolution_convert_fusion.2), channel_id=1, source_target_pairs={{0,8},{8,0},{1,9},{9,1},{2,10},{10,2},{3,11},{11,3},{4,12},{12,4},... | collective-permute-start | bytes 6291464 | tf_op jit(solution)/shard_map/ppermute | solution.py:27
  93.0 2.0 %collective-permute-start.2 = (bf16[2,1024,128]{2,1,0:T(8,128)(2,1)S(1)}, bf16[2,1024,128]{2,1,0:T(8,128)(2,1)S(1)}, u32[]{:S(2)}, u32[]{:S(2)}) collective-permute-start(bf16[2,1024,128]{2,1,0:T(8,128)(2,1)S(1)} %fusion.16), channel_id=1, source_target_pairs={{0,8},{8,0},{1,9},{9,1},{2,10},{10,2},{3,11},{11,3},{4,12},{12,4},... | collective-permute-start | bytes 1572872 | tf_op jit(solution)/shard_map/ppermute | solution.py:27
  98.0 40.4 %all-to-all-start.2 = ((bf16[32,320,128]{2,1,0:T(8,128)(2,1)}), bf16[32,320,128]{2,1,0:T(8,128)(2,1)S(1)}, u32[]{:S(2)}, u32[]{:S(2)}) async-start(bf16[32,320,128]{2,1,0:T(8,128)(2,1)} %bitcast.122), calls=%async_computation.2 | async-start | bytes 5242880 | tf_op jit(solution)/shard_map/all_to_all | solution.py:115
  105.0 60.7 %copy-start.1 = (bf16[512,128]{1,0:T(8,128)(2,1)S(1)}, bf16[512,128]{1,0:T(8,128)(2,1)}, u32[]{:S(2)}) copy-start(bf16[512,128]{1,0:T(8,128)(2,1)} %param.15) | copy-start | bytes 393220
  138.5 14.2 %all-to-all-start.4 = ((bf16[8,64,128]{2,1,0:T(8,128)(2,1)}), bf16[8,64,128]{2,1,0:T(8,128)(2,1)S(1)}, u32[]{:S(2)}, u32[]{:S(2)}) async-start(bf16[8,64,128]{2,1,0:T(8,128)(2,1)} %fusion.19), calls=%async_computation.4 | async-start | bytes 262144 | tf_op jit(solution)/shard_map/all_to_all | solution.py:120
  152.7 11.9 %all-to-all-start.3 = ((f32[4,80,128]{2,1,0:T(8,128)}), f32[4,80,128]{2,1,0:T(8,128)S(1)}, u32[]{:S(2)}, u32[]{:S(2)}) async-start(f32[4,80,128]{2,1,0:T(8,128)} %bitcast.39), calls=%async_computation.3 | async-start | bytes 327680 | tf_op jit(solution)/shard_map/all_to_all | solution.py:124
